TPU v7x, 512 devices: a whole 4x4x16 slice. The times are simulated.
512 devices in a mesh: band: 16 (over x, z_hi, core), col: 32 (over z_lo, y).
Axes of the slice: x: 4, y: 4, z: 16 (z_hi: 2, z_lo: 8; z = z_hi * 8 + z_lo), core: 2. Of those that a mesh axis runs over, the one named last changes fastest.
Arguments:
- left_image: bfloat16 [64, 4096, 256], P('band', 'col'), may hold values from -6 to 6
- right_image: bfloat16 [64, 4096, 256], P('band', 'col'), may hold values from -6 to 6
- kernel: bfloat16 [2304, 256], replicated, may hold values from -0.125 to 0.125
- valid_mask: int32 [64, 4096], P('band', 'col'), may hold values 0 or 1
- disparity: int32 [64, 4096], P('band', 'col'), may hold values from 0 to 511
Outputs:
- grad_left: bfloat16 [64, 4096, 256], P('band', 'col')
- grad_right: bfloat16 [64, 4096, 256], P('band', 'col')
All inputs are finite; a program needn't handle non-finite values. No bound on the sum of `valid_mask` on one device may be relied on, other than what follows from the above.
Results may differ from a plain program's by a relative error of at most 0.011.
Values may be sent and summed in bfloat16 or wider, within the bound.
No kernel may reach another device: no remote copies, remote signals or barrier semaphores. Data moves between devices by JAX's collectives and lax.ppermute only.
A program may use at most 64 MiB of HBM per device.

v0:
```python
import jax
import jax.numpy as jnp
from jax import lax
from jax.sharding import PartitionSpec as P

DISP = 512


def extended(block, sides, width):
    for axis, dim in sides:
        count = lax.axis_size(axis)
        forward = [(i, i + 1) for i in range(count - 1)]
        backward = [(target, source) for source, target in forward]
        low = lax.ppermute(
            lax.slice_in_dim(block, block.shape[dim] - width, None, axis=dim), axis, forward
        )
        high = lax.ppermute(lax.slice_in_dim(block, 0, width, axis=dim), axis, backward)
        block = jnp.concatenate([low, block, high], axis=dim)
    return block


def passed_along(value, axis, steps):
    count = lax.axis_size(axis)
    leading, last = (max(0, -steps), min(count, count - steps))
    return lax.ppermute(value, axis, [(source, source + steps) for source in range(leading, last)])


def conv_pair(padded, weights):
    pairs = padded.shape[0]
    height = padded.shape[1] - 2
    columns = padded.shape[2] - 2
    channels = padded.shape[3]
    pieces = [
        padded[:, row_off : row_off + height, col_off : col_off + columns]
        for row_off in range(3)
        for col_off in range(3)
    ]
    patches = jnp.concatenate(pieces, axis=3).reshape(pairs * height * columns, 9 * channels)
    result = jnp.dot(patches, weights, preferred_element_type=jnp.float32)
    return result.reshape(pairs, height, columns, weights.shape[1])


def band_to_diagonals(scores, reach):
    height, columns, extent = scores.shape
    flattened = scores.reshape(height, columns * extent)
    flattened = jnp.concatenate([flattened, jnp.zeros((height, columns), scores.dtype)], 1)
    return flattened.reshape(height, columns, extent + 1)[:, :, 1 : reach + 1]


def diagonals_to_band(reversed_rows, reach):
    height, columns, _ = reversed_rows.shape
    extent = columns + reach
    widened = jnp.concatenate(
        [
            jnp.zeros((height, columns, 1), reversed_rows.dtype),
            reversed_rows,
            jnp.zeros((height, columns, columns), reversed_rows.dtype),
        ],
        2,
    )
    flattened = widened.reshape(height, columns * (extent + 1))[:, : columns * extent]
    return flattened.reshape(height, columns, extent)


def shards(left_image, right_image, kernel, valid_mask, disparity):
    columns = left_image.shape[1]
    channels = left_image.shape[2]
    reach_devs = DISP // columns
    factor = channels ** (-0.5)
    stacked = jnp.stack((left_image, right_image), 0)
    rimmed = extended(stacked, (("band", 1), ("col", 2)), 1)
    features = conv_pair(rimmed, kernel).astype(jnp.bfloat16)
    left_feat = features[0]
    right_feat = features[1]
    received = [
        passed_along(right_feat, "col", reach_devs - position) for position in range(reach_devs)
    ]
    segment = jnp.concatenate(received + [right_feat], 1)
    scores = (
        jnp.einsum("rxc,ryc->rxy", left_feat, segment, preferred_element_type=jnp.float32) * factor
    )
    correlation = band_to_diagonals(scores, DISP)[:, :, ::-1]
    disparities = jnp.arange(DISP, dtype=jnp.int32)
    distance = (disparities[None, None, :] - disparity[:, :, None]).astype(jnp.float32)
    target = jnp.exp(-distance * distance / 8.0)
    validity = valid_mask.astype(jnp.float32)[:, :, None]
    gradient = (validity * (correlation - target) * (channels / DISP)).astype(jnp.bfloat16)
    banded = diagonals_to_band(gradient[:, :, ::-1], DISP)
    left_term = (
        jnp.einsum("rxy,ryc->rxc", banded, segment, preferred_element_type=jnp.float32) * factor
    )
    segment_term = (
        jnp.einsum("rxy,rxc->ryc", banded, left_feat, preferred_element_type=jnp.float32) * factor
    )
    pieces = [
        segment_term[:, position * columns : (position + 1) * columns]
        for position in range(reach_devs)
    ]
    own_part = segment_term[:, reach_devs * columns :]
    summed = own_part
    for position in range(reach_devs):
        summed = summed + passed_along(
            pieces[position].astype(jnp.bfloat16), "col", position - reach_devs
        ).astype(jnp.float32)
    grads = jnp.stack((left_term.astype(jnp.bfloat16), summed.astype(jnp.bfloat16)), 0)
    grad_padded = extended(grads, (("band", 1), ("col", 2)), 1)
    blocks = kernel.reshape(3, 3, channels, channels)[::-1, ::-1]
    flipped = jnp.transpose(blocks, (0, 1, 3, 2)).reshape(9 * channels, channels)
    outputs = conv_pair(grad_padded, flipped).astype(jnp.bfloat16)
    return (outputs[0], outputs[1])


def solution(mesh):
    return jax.shard_map(
        shards,
        mesh=mesh,
        in_specs=(
            P("band", "col", None),
            P("band", "col", None),
            P(),
            P("band", "col"),
            P("band", "col"),
        ),
        out_specs=(P("band", "col", None), P("band", "col", None)),
        check_vma=False,
    )
```

profile of v0, /device:TPU:5, one launch (start us, length us, event | category | flops | bytes accessed | tf_op | source)
XLA Modules:
  0.0 149.0 jit_solution(7006102273406548219)
XLA Ops:
  0.6 0.0 copy-start
  0.6 0.0 copy-start.1
  0.7 1.0 fusion.27
  1.7 16.0 %collective-permute-start = (bf16[2,1,128,256]{3,2,1,0:T(8,128)(2,1)S(1)}, bf16[2,1,128,256]{3,2,1,0:T(8,128)(2,1)S(1)}, u32[]{:S(2)}, u32[]{:S(2)}) collective-permute-start(bf16[2,1,128,256]{3,2,1,0:T(8,128)(2,1)S(1)} %get-tuple-element.18), channel_id=1, source_target_pairs={{0,32},{32,64},{64,96},{96,128},{128,160},{160,192},{192,224},{224... | collective-permute-start | bytes 393224 | tf_op jit(solution)/shard_map/ppermute | solution.py:14
  17.7 1.9 %collective-permute-start.1 = (bf16[2,1,128,256]{3,2,1,0:T(8,128)(2,1)S(1)}, bf16[2,1,128,256]{3,2,1,0:T(8,128)(2,1)S(1)}, u32[]{:S(2)}, u32[]{:S(2)}) collective-permute-start(bf16[2,1,128,256]{3,2,1,0:T(8,128)(2,1)S(1)} %get-tuple-element.19), channel_id=1, source_target_pairs={{32,0},{64,32},{96,64},{128,96},{160,128},{192,160},{224,192},{256... | collective-permute-start | bytes 393224 | tf_op jit(solution)/shard_map/ppermute | solution.py:17
  19.6 3.5 %collective-permute-done = bf16[2,1,128,256]{3,2,1,0:T(8,128)(2,1)S(1)} collective-permute-done((bf16[2,1,128,256]{3,2,1,0:T(8,128)(2,1)S(1)}, bf16[2,1,128,256]{3,2,1,0:T(8,128)(2,1)S(1)}, u32[]{:S(2)}, u32[]{:S(2)}) %collective-permute-start) | collective-permute-done | bytes 131104 | tf_op jit(solution)/shard_map/ppermute | solution.py:14
  23.1 11.1 %collective-permute-done.1 = bf16[2,1,128,256]{3,2,1,0:T(8,128)(2,1)S(1)} collective-permute-done((bf16[2,1,128,256]{3,2,1,0:T(8,128)(2,1)S(1)}, bf16[2,1,128,256]{3,2,1,0:T(8,128)(2,1)S(1)}, u32[]{:S(2)}, u32[]{:S(2)}) %collective-permute-start.1) | collective-permute-done | bytes 131104 | tf_op jit(solution)/shard_map/ppermute | solution.py:17
  34.2 0.8 pad_maximum_fusion.16
  35.0 3.2 %collective-permute-start.2 = (bf16[2,6,1,256]{3,2,1,0:T(2,128)(2,1)S(1)}, bf16[2,6,1,256]{3,2,1,0:T(2,128)(2,1)S(1)}, u32[]{:S(2)}, u32[]{:S(2)}) collective-permute-start(bf16[2,6,1,256]{3,2,1,0:T(2,128)(2,1)S(1)} %get-tuple-element.13), channel_id=1, source_target_pairs={{0,1},{1,2},{2,3},{3,4},{4,5},{5,6},{6,7},{7,8},{8,9},{9,10},{10,1... | collective-permute-start | bytes 18440 | tf_op jit(solution)/shard_map/ppermute | solution.py:14
  38.2 1.3 collective-permute-start.3
  39.5 3.1 %collective-permute-done.3 = bf16[2,6,1,256]{3,2,1,0:T(2,128)(2,1)S(1)} collective-permute-done((bf16[2,6,1,256]{3,2,1,0:T(2,128)(2,1)S(1)}, bf16[2,6,1,256]{3,2,1,0:T(2,128)(2,1)S(1)}, u32[]{:S(2)}, u32[]{:S(2)}) %collective-permute-start.3) | collective-permute-done | bytes 6176 | tf_op jit(solution)/shard_map/ppermute | solution.py:17
  42.7 0.3 pad_maximum_fusion
  43.1 0.1 slice_dynamic-update-slice_fusion.10
  43.3 0.1 slice_dynamic-update-slice_fusion.8
  43.6 0.1 slice_dynamic-update-slice_fusion.6
  43.7 1.0 copy-done.4
  44.8 1.4 convolution_convert_fusion.1
  46.2 3.7 %collective-permute-start.4 = (bf16[4,128,256]{2,1,0:T(8,128)(2,1)S(1)}, bf16[4,128,256]{2,1,0:T(8,128)(2,1)S(1)}, u32[]{:S(2)}, u32[]{:S(2)}) collective-permute-start(bf16[4,128,256]{2,1,0:T(8,128)(2,1)S(1)} %slice_bitcast_fusion.2), channel_id=1, source_target_pairs={{0,4},{1,5},{2,6},{3,7},{4,8},{5,9},{6,10},{7,11},{8,12},{9,13},{1... | collective-permute-start | bytes 786440 | tf_op jit(solution)/shard_map/ppermute | solution.py:25
  49.8 7.1 %collective-permute-start.5 = (bf16[4,128,256]{2,1,0:T(8,128)(2,1)S(1)}, bf16[4,128,256]{2,1,0:T(8,128)(2,1)S(1)}, u32[]{:S(2)}, u32[]{:S(2)}) collective-permute-start(bf16[4,128,256]{2,1,0:T(8,128)(2,1)S(1)} %slice_bitcast_fusion.2), channel_id=1, source_target_pairs={{0,3},{1,4},{2,5},{3,6},{4,7},{5,8},{6,9},{7,10},{8,11},{9,12},{10... | collective-permute-start | bytes 786440 | tf_op jit(solution)/shard_map/ppermute | solution.py:25
  56.9 1.5 %collective-permute-start.6 = (bf16[4,128,256]{2,1,0:T(8,128)(2,1)S(1)}, bf16[4,128,256]{2,1,0:T(8,128)(2,1)S(1)}, u32[]{:S(2)}, u32[]{:S(2)}) collective-permute-start(bf16[4,128,256]{2,1,0:T(8,128)(2,1)S(1)} %slice_bitcast_fusion.2), channel_id=1, source_target_pairs={{0,2},{1,3},{2,4},{3,5},{4,6},{5,7},{6,8},{7,9},{8,10},{9,11},{10,... | collective-permute-start | bytes 786440 | tf_op jit(solution)/shard_map/ppermute | solution.py:25
  58.4 0.1 pad.27.clone
  58.5 2.9 %collective-permute-start.7 = (bf16[4,128,256]{2,1,0:T(8,128)(2,1)S(1)}, bf16[4,128,256]{2,1,0:T(8,128)(2,1)S(1)}, u32[]{:S(2)}, u32[]{:S(2)}) collective-permute-start(bf16[4,128,256]{2,1,0:T(8,128)(2,1)S(1)} %slice_bitcast_fusion.2), channel_id=1, source_target_pairs={{0,1},{1,2},{2,3},{3,4},{4,5},{5,6},{6,7},{7,8},{8,9},{9,10},{10,1... | collective-permute-start | bytes 786440 | tf_op jit(solution)/shard_map/ppermute | solution.py:25
  61.5 1.5 %collective-permute-done.5 = bf16[4,128,256]{2,1,0:T(8,128)(2,1)S(1)} collective-permute-done((bf16[4,128,256]{2,1,0:T(8,128)(2,1)S(1)}, bf16[4,128,256]{2,1,0:T(8,128)(2,1)S(1)}, u32[]{:S(2)}, u32[]{:S(2)}) %collective-permute-start.5) | collective-permute-done | bytes 262176 | tf_op jit(solution)/shard_map/ppermute | solution.py:25
  63.1 1.7 %collective-permute-done.7 = bf16[4,128,256]{2,1,0:T(8,128)(2,1)S(1)} collective-permute-done((bf16[4,128,256]{2,1,0:T(8,128)(2,1)S(1)}, bf16[4,128,256]{2,1,0:T(8,128)(2,1)S(1)}, u32[]{:S(2)}, u32[]{:S(2)}) %collective-permute-start.7) | collective-permute-done | bytes 262176 | tf_op jit(solution)/shard_map/ppermute | solution.py:25
  64.8 1.1 copy-done.2
  65.9 0.5 fusion
  66.4 0.8 copy.14
  67.2 0.2 concatenate.62
  67.5 1.6 %reshape.33 = f32[4,128,641]{2,1,0:T(8,128)S(1)} reshape(f32[4,82048]{1,0:T(4,128)S(1)} %concatenate.62) | data formatting | bytes 2625536 | tf_op jit(solution)/shard_map/reshape | solution.py:47
  69.1 0.0 copy-start.6
  69.1 0.3 slice.172
  69.4 1.5 %rev.9 = f32[4,128,512]{2,1,0:T(8,128)S(1)} reverse(f32[4,128,512]{2,1,0:T(8,128)S(1)} %slice.172), dimensions={2} | reverse | bytes 2097152 | tf_op jit(solution)/shard_map/rev | solution.py:82
  70.9 0.0 copy-done.6
  71.0 0.4 fusion.9
  71.4 1.6 %rev.10 = bf16[4,128,512]{2,1,0:T(8,128)(2,1)S(1)} reverse(bf16[4,128,512]{2,1,0:T(8,128)(2,1)S(1)} %fusion.9), dimensions={2} | reverse | bytes 1048576 | tf_op jit(solution)/shard_map/rev | solution.py:88
  73.1 0.4 maximum_maximum_fusion.2
  73.5 1.6 %reshape.34 = bf16[4,82048]{1,0:T(4,128)(2,1)S(1)} reshape(bf16[4,128,641]{2,1,0:T(8,128)(2,1)S(1)} %maximum_maximum_fusion.2) | data formatting | bytes 1312768 | tf_op jit(solution)/shard_map/reshape | solution.py:61
  75.0 0.2 slice.173
  75.3 0.6 fusion.30
  75.9 0.1 fusion.29
  75.9 1.4 collective-permute-start.10
  77.4 1.3 collective-permute-start.11
  78.7 1.3 collective-permute-start.8
  80.0 1.3 collective-permute-start.9
  81.3 0.4 fusion.3
  81.7 4.4 %collective-permute-done.10 = bf16[4,128,256]{2,1,0:T(8,128)(2,1)S(1)} collective-permute-done((bf16[4,128,256]{2,1,0:T(8,128)(2,1)S(1)}, bf16[4,128,256]{2,1,0:T(8,128)(2,1)S(1)}, u32[]{:S(2)}, u32[]{:S(2)}) %collective-permute-start.10) | collective-permute-done | bytes 262176 | tf_op jit(solution)/shard_map/ppermute | solution.py:25
  86.1 3.1 %collective-permute-done.11 = bf16[4,128,256]{2,1,0:T(8,128)(2,1)S(1)} collective-permute-done((bf16[4,128,256]{2,1,0:T(8,128)(2,1)S(1)}, bf16[4,128,256]{2,1,0:T(8,128)(2,1)S(1)}, u32[]{:S(2)}, u32[]{:S(2)}) %collective-permute-start.11) | collective-permute-done | bytes 262176 | tf_op jit(solution)/shard_map/ppermute | solution.py:25
  89.2 13.1 %collective-permute-done.8 = bf16[4,128,256]{2,1,0:T(8,128)(2,1)S(1)} collective-permute-done((bf16[4,128,256]{2,1,0:T(8,128)(2,1)S(1)}, bf16[4,128,256]{2,1,0:T(8,128)(2,1)S(1)}, u32[]{:S(2)}, u32[]{:S(2)}) %collective-permute-start.8) | collective-permute-done | bytes 262176 | tf_op jit(solution)/shard_map/ppermute | solution.py:25
  102.4 0.2 fusion.24
  102.6 14.3 %collective-permute-start.12 = (bf16[2,1,128,256]{3,2,1,0:T(8,128)(2,1)S(1)}, bf16[2,1,128,256]{3,2,1,0:T(8,128)(2,1)S(1)}, u32[]{:S(2)}, u32[]{:S(2)}) collective-permute-start(bf16[2,1,128,256]{3,2,1,0:T(8,128)(2,1)S(1)} %get-tuple-element.16), channel_id=1, source_target_pairs={{0,32},{32,64},{64,96},{96,128},{128,160},{160,192},{192,224},{224... | collective-permute-start | bytes 393224 | tf_op jit(solution)/shard_map/ppermute | solution.py:14
  116.8 1.9 %collective-permute-start.13 = (bf16[2,1,128,256]{3,2,1,0:T(8,128)(2,1)S(1)}, bf16[2,1,128,256]{3,2,1,0:T(8,128)(2,1)S(1)}, u32[]{:S(2)}, u32[]{:S(2)}) collective-permute-start(bf16[2,1,128,256]{3,2,1,0:T(8,128)(2,1)S(1)} %get-tuple-element.17), channel_id=1, source_target_pairs={{32,0},{64,32},{96,64},{128,96},{160,128},{192,160},{224,192},{256... | collective-permute-start | bytes 393224 | tf_op jit(solution)/shard_map/ppermute | solution.py:17
  118.8 4.3 %collective-permute-done.12 = bf16[2,1,128,256]{3,2,1,0:T(8,128)(2,1)S(1)} collective-permute-done((bf16[2,1,128,256]{3,2,1,0:T(8,128)(2,1)S(1)}, bf16[2,1,128,256]{3,2,1,0:T(8,128)(2,1)S(1)}, u32[]{:S(2)}, u32[]{:S(2)}) %collective-permute-start.12) | collective-permute-done | bytes 131104 | tf_op jit(solution)/shard_map/ppermute | solution.py:14
  123.1 10.2 %collective-permute-done.13 = bf16[2,1,128,256]{3,2,1,0:T(8,128)(2,1)S(1)} collective-permute-done((bf16[2,1,128,256]{3,2,1,0:T(8,128)(2,1)S(1)}, bf16[2,1,128,256]{3,2,1,0:T(8,128)(2,1)S(1)}, u32[]{:S(2)}, u32[]{:S(2)}) %collective-permute-start.13) | collective-permute-done | bytes 131104 | tf_op jit(solution)/shard_map/ppermute | solution.py:17
  133.3 8.0 %collective-permute-start.14 = (bf16[2,6,1,256]{3,2,1,0:T(2,128)(2,1)S(1)}, bf16[2,6,1,256]{3,2,1,0:T(2,128)(2,1)S(1)}, u32[]{:S(2)}, u32[]{:S(2)}) collective-permute-start(bf16[2,6,1,256]{3,2,1,0:T(2,128)(2,1)S(1)} %get-tuple-element.9), channel_id=1, source_target_pairs={{0,1},{1,2},{2,3},{3,4},{4,5},{5,6},{6,7},{7,8},{8,9},{9,10},{10,1... | collective-permute-start | bytes 18440 | tf_op jit(solution)/shard_map/ppermute | solution.py:14
  141.3 1.5 collective-permute-start.15
  142.8 0.1 reverse_bitcast_fusion
  142.9 0.7 copy.10
  143.6 2.1 %collective-permute-done.15 = bf16[2,6,1,256]{3,2,1,0:T(2,128)(2,1)S(1)} collective-permute-done((bf16[2,6,1,256]{3,2,1,0:T(2,128)(2,1)S(1)}, bf16[2,6,1,256]{3,2,1,0:T(2,128)(2,1)S(1)}, u32[]{:S(2)}, u32[]{:S(2)}) %collective-permute-start.15) | collective-permute-done | bytes 6176 | tf_op jit(solution)/shard_map/ppermute | solution.py:17
  145.7 0.3 pad_maximum_fusion.1
  146.1 0.1 slice_dynamic-update-slice_fusion.4
  146.4 0.1 slice_dynamic-update-slice_fusion.2
  146.6 0.1 slice_dynamic-update-slice_fusion
  146.7 1.4 convolution_convert_fusion
  148.1 0.8 slice_bitcast_fusion
  (38 shorter events, 0.6 us)
Async XLA Ops:
  0.6 42.0 %copy-start = (bf16[4,128,256]{2,1,0:T(8,128)(2,1)S(1)}, bf16[4,128,256]{2,1,0:T(8,128)(2,1)}, u32[]{:S(2)}) copy-start(bf16[4,128,256]{2,1,0:T(8,128)(2,1)} %param.5) | copy-start | bytes 786436
  0.6 42.0 %copy-start.1 = (bf16[4,128,256]{2,1,0:T(8,128)(2,1)S(1)}, bf16[4,128,256]{2,1,0:T(8,128)(2,1)}, u32[]{:S(2)}) copy-start(bf16[4,128,256]{2,1,0:T(8,128)(2,1)} %param.6) | copy-start | bytes 786436
  1.7 21.5 %collective-permute-start = (bf16[2,1,128,256]{3,2,1,0:T(8,128)(2,1)S(1)}, bf16[2,1,128,256]{3,2,1,0:T(8,128)(2,1)S(1)}, u32[]{:S(2)}, u32[]{:S(2)}) collective-permute-start(bf16[2,1,128,256]{3,2,1,0:T(8,128)(2,1)S(1)} %get-tuple-element.18), channel_id=1, source_target_pairs={{0,32},{32,64},{64,96},{96,128},{128,160},{160,192},{192,224},{224... | collective-permute-start | bytes 393224 | tf_op jit(solution)/shard_map/ppermute | solution.py:14
  17.7 16.5 %collective-permute-start.1 = (bf16[2,1,128,256]{3,2,1,0:T(8,128)(2,1)S(1)}, bf16[2,1,128,256]{3,2,1,0:T(8,128)(2,1)S(1)}, u32[]{:S(2)}, u32[]{:S(2)}) collective-permute-start(bf16[2,1,128,256]{3,2,1,0:T(8,128)(2,1)S(1)} %get-tuple-element.19), channel_id=1, source_target_pairs={{32,0},{64,32},{96,64},{128,96},{160,128},{192,160},{224,192},{256... | collective-permute-start | bytes 393224 | tf_op jit(solution)/shard_map/ppermute | solution.py:17
  35.0 4.5 %collective-permute-start.2 = (bf16[2,6,1,256]{3,2,1,0:T(2,128)(2,1)S(1)}, bf16[2,6,1,256]{3,2,1,0:T(2,128)(2,1)S(1)}, u32[]{:S(2)}, u32[]{:S(2)}) collective-permute-start(bf16[2,6,1,256]{3,2,1,0:T(2,128)(2,1)S(1)} %get-tuple-element.13), channel_id=1, source_target_pairs={{0,1},{1,2},{2,3},{3,4},{4,5},{5,6},{6,7},{7,8},{8,9},{9,10},{10,1... | collective-permute-start | bytes 18440 | tf_op jit(solution)/shard_map/ppermute | solution.py:14
  38.2 4.4 %collective-permute-start.3 = (bf16[2,6,1,256]{3,2,1,0:T(2,128)(2,1)S(1)}, bf16[2,6,1,256]{3,2,1,0:T(2,128)(2,1)S(1)}, u32[]{:S(2)}, u32[]{:S(2)}) collective-permute-start(bf16[2,6,1,256]{3,2,1,0:T(2,128)(2,1)S(1)} %get-tuple-element.12), channel_id=1, source_target_pairs={{1,0},{2,1},{3,2},{4,3},{5,4},{6,5},{7,6},{8,7},{9,8},{10,9},{11,1... | collective-permute-start | bytes 18440 | tf_op jit(solution)/shard_map/ppermute | solution.py:17
  43.5 1.3 copy-start.4
  44.8 13.7 %copy-start.7 = (s32[4,128]{1,0:T(4,128)S(1)}, s32[4,128]{1,0:T(4,128)}, u32[]{:S(2)}) copy-start(s32[4,128]{1,0:T(4,128)} %param.8) | copy-start | bytes 6148
  46.2 15.3 %collective-permute-start.4 = (bf16[4,128,256]{2,1,0:T(8,128)(2,1)S(1)}, bf16[4,128,256]{2,1,0:T(8,128)(2,1)S(1)}, u32[]{:S(2)}, u32[]{:S(2)}) collective-permute-start(bf16[4,128,256]{2,1,0:T(8,128)(2,1)S(1)} %slice_bitcast_fusion.2), channel_id=1, source_target_pairs={{0,4},{1,5},{2,6},{3,7},{4,8},{5,9},{6,10},{7,11},{8,12},{9,13},{1... | collective-permute-start | bytes 786440 | tf_op jit(solution)/shard_map/ppermute | solution.py:25
  49.8 13.2 %collective-permute-start.5 = (bf16[4,128,256]{2,1,0:T(8,128)(2,1)S(1)}, bf16[4,128,256]{2,1,0:T(8,128)(2,1)S(1)}, u32[]{:S(2)}, u32[]{:S(2)}) collective-permute-start(bf16[4,128,256]{2,1,0:T(8,128)(2,1)S(1)} %slice_bitcast_fusion.2), channel_id=1, source_target_pairs={{0,3},{1,4},{2,5},{3,6},{4,7},{5,8},{6,9},{7,10},{8,11},{9,12},{10... | collective-permute-start | bytes 786440 | tf_op jit(solution)/shard_map/ppermute | solution.py:25
  56.9 6.1 %collective-permute-start.6 = (bf16[4,128,256]{2,1,0:T(8,128)(2,1)S(1)}, bf16[4,128,256]{2,1,0:T(8,128)(2,1)S(1)}, u32[]{:S(2)}, u32[]{:S(2)}) collective-permute-start(bf16[4,128,256]{2,1,0:T(8,128)(2,1)S(1)} %slice_bitcast_fusion.2), channel_id=1, source_target_pairs={{0,2},{1,3},{2,4},{3,5},{4,6},{5,7},{6,8},{7,9},{8,10},{9,11},{10,... | collective-permute-start | bytes 786440 | tf_op jit(solution)/shard_map/ppermute | solution.py:25
  58.5 6.2 %collective-permute-start.7 = (bf16[4,128,256]{2,1,0:T(8,128)(2,1)S(1)}, bf16[4,128,256]{2,1,0:T(8,128)(2,1)S(1)}, u32[]{:S(2)}, u32[]{:S(2)}) collective-permute-start(bf16[4,128,256]{2,1,0:T(8,128)(2,1)S(1)} %slice_bitcast_fusion.2), channel_id=1, source_target_pairs={{0,1},{1,2},{2,3},{3,4},{4,5},{5,6},{6,7},{7,8},{8,9},{9,10},{10,1... | collective-permute-start | bytes 786440 | tf_op jit(solution)/shard_map/ppermute | solution.py:25
  64.8 1.1 copy-start.2
  69.1 1.8 %copy-start.6 = (s32[4,128]{1,0:T(4,128)S(1)}, s32[4,128]{1,0:T(4,128)}, u32[]{:S(2)}) copy-start(s32[4,128]{1,0:T(4,128)} %param.9) | copy-start | bytes 6148
  75.8 5.4 %copy-start.3 = (bf16[4,640,256]{2,1,0:T(8,128)(2,1)S(1)}, bf16[4,640,256]{2,1,0:T(8,128)(2,1)}, u32[]{:S(2)}) copy-start(bf16[4,640,256]{2,1,0:T(8,128)(2,1)} %copy-done.2) | copy-start | bytes 3932164
  75.9 10.1 %collective-permute-start.10 = (bf16[4,128,256]{2,1,0:T(8,128)(2,1)S(1)}, bf16[4,128,256]{2,1,0:T(8,128)(2,1)S(1)}, u32[]{:S(2)}, u32[]{:S(2)}) collective-permute-start(bf16[4,128,256]{2,1,0:T(8,128)(2,1)S(1)} %get-tuple-element.4), channel_id=1, source_target_pairs={{2,0},{3,1},{4,2},{5,3},{6,4},{7,5},{8,6},{9,7},{10,8},{11,9},{12,... | collective-permute-start | bytes 786440 | tf_op jit(solution)/shard_map/ppermute | solution.py:25
  77.4 11.8 %collective-permute-start.11 = (bf16[4,128,256]{2,1,0:T(8,128)(2,1)S(1)}, bf16[4,128,256]{2,1,0:T(8,128)(2,1)S(1)}, u32[]{:S(2)}, u32[]{:S(2)}) collective-permute-start(bf16[4,128,256]{2,1,0:T(8,128)(2,1)S(1)} %get-tuple-element.3), channel_id=1, source_target_pairs={{1,0},{2,1},{3,2},{4,3},{5,4},{6,5},{7,6},{8,7},{9,8},{10,9},{11,1... | collective-permute-start | bytes 786440 | tf_op jit(solution)/shard_map/ppermute | solution.py:25
  78.7 23.7 %collective-permute-start.8 = (bf16[4,128,256]{2,1,0:T(8,128)(2,1)S(1)}, bf16[4,128,256]{2,1,0:T(8,128)(2,1)S(1)}, u32[]{:S(2)}, u32[]{:S(2)}) collective-permute-start(bf16[4,128,256]{2,1,0:T(8,128)(2,1)S(1)} %get-tuple-element.2), channel_id=1, source_target_pairs={{4,0},{5,1},{6,2},{7,3},{8,4},{9,5},{10,6},{11,7},{12,8},{13,9},{1... | collective-permute-start | bytes 786440 | tf_op jit(solution)/shard_map/ppermute | solution.py:25
  80.0 22.4 %collective-permute-start.9 = (bf16[4,128,256]{2,1,0:T(8,128)(2,1)S(1)}, bf16[4,128,256]{2,1,0:T(8,128)(2,1)S(1)}, u32[]{:S(2)}, u32[]{:S(2)}) collective-permute-start(bf16[4,128,256]{2,1,0:T(8,128)(2,1)S(1)} %get-tuple-element.5), channel_id=1, source_target_pairs={{3,0},{4,1},{5,2},{6,3},{7,4},{8,5},{9,6},{10,7},{11,8},{12,9},{13... | collective-permute-start | bytes 786440 | tf_op jit(solution)/shard_map/ppermute | solution.py:25
  102.4 40.4 %copy-start.5 = (bf16[2304,256]{1,0:T(8,128)(2,1)S(1)}, bf16[2304,256]{1,0:T(8,128)(2,1)}, u32[]{:S(2)}) copy-start(bf16[2304,256]{1,0:T(8,128)(2,1)} %param.7) | copy-start | bytes 3538948
  102.6 20.5 %collective-permute-start.12 = (bf16[2,1,128,256]{3,2,1,0:T(8,128)(2,1)S(1)}, bf16[2,1,128,256]{3,2,1,0:T(8,128)(2,1)S(1)}, u32[]{:S(2)}, u32[]{:S(2)}) collective-permute-start(bf16[2,1,128,256]{3,2,1,0:T(8,128)(2,1)S(1)} %get-tuple-element.16), channel_id=1, source_target_pairs={{0,32},{32,64},{64,96},{96,128},{128,160},{160,192},{192,224},{224... | collective-permute-start | bytes 393224 | tf_op jit(solution)/shard_map/ppermute | solution.py:14
  116.8 16.5 %collective-permute-start.13 = (bf16[2,1,128,256]{3,2,1,0:T(8,128)(2,1)S(1)}, bf16[2,1,128,256]{3,2,1,0:T(8,128)(2,1)S(1)}, u32[]{:S(2)}, u32[]{:S(2)}) collective-permute-start(bf16[2,1,128,256]{3,2,1,0:T(8,128)(2,1)S(1)} %get-tuple-element.17), channel_id=1, source_target_pairs={{32,0},{64,32},{96,64},{128,96},{160,128},{192,160},{224,192},{256... | collective-permute-start | bytes 393224 | tf_op jit(solution)/shard_map/ppermute | solution.py:17
  133.3 10.3 %collective-permute-start.14 = (bf16[2,6,1,256]{3,2,1,0:T(2,128)(2,1)S(1)}, bf16[2,6,1,256]{3,2,1,0:T(2,128)(2,1)S(1)}, u32[]{:S(2)}, u32[]{:S(2)}) collective-permute-start(bf16[2,6,1,256]{3,2,1,0:T(2,128)(2,1)S(1)} %get-tuple-element.9), channel_id=1, source_target_pairs={{0,1},{1,2},{2,3},{3,4},{4,5},{5,6},{6,7},{7,8},{8,9},{9,10},{10,1... | collective-permute-start | bytes 18440 | tf_op jit(solution)/shard_map/ppermute | solution.py:14
  141.3 4.4 %collective-permute-start.15 = (bf16[2,6,1,256]{3,2,1,0:T(2,128)(2,1)S(1)}, bf16[2,6,1,256]{3,2,1,0:T(2,128)(2,1)S(1)}, u32[]{:S(2)}, u32[]{:S(2)}) collective-permute-start(bf16[2,6,1,256]{3,2,1,0:T(2,128)(2,1)S(1)} %get-tuple-element.8), channel_id=1, source_target_pairs={{1,0},{2,1},{3,2},{4,3},{5,4},{6,5},{7,6},{8,7},{9,8},{10,9},{11,1... | collective-permute-start | bytes 18440 | tf_op jit(solution)/shard_map/ppermute | solution.py:17
where the time goes:
time: 150 us; the launch traced here: 149 us
  starting transfers between devices  68.4 us (46%)
  waiting for transfers between devices  58.3 us (39%)
  local copies, waits for them, and re-layouts  13.1 us (9%)
  matrix products  4.22 us (3%)
  other arithmetic  3.76 us (3%)
    ppermute x4, starting transfers between devices, extended(): lax.ppermute(lax.slice_in_dim(block, block.shape[dim] - width, None, axis...  41.4 us
    ppermute x4, waiting for transfers between devices, extended(): lax.ppermute(lax.slice_in_dim(block, 0, width, axis=dim), axis, backward)  26.6 us
    ppermute x8, waiting for transfers between devices, passed_along(): lax.ppermute(value, axis, [(source, source + steps) for source in range(l...  23.9 us
    ppermute x8, starting transfers between devices, passed_along(): lax.ppermute(value, axis, [(source, source + steps) for source in range(l...  20.4 us
    ppermute x4, waiting for transfers between devices, extended(): lax.ppermute(lax.slice_in_dim(block, block.shape[dim] - width, None, axis...  7.81 us
    ppermute x4, starting transfers between devices, extended(): lax.ppermute(lax.slice_in_dim(block, 0, width, axis=dim), axis, backward)  6.61 us
    unnamed x31, local copies, waits for them, and re-layouts  3.82 us
  transfers between devices with their start and end apart: 16, of which 11 were waited for; matrix products, arithmetic and copies ran while one was open for 1% of the time, Pallas kernels for 0%

commit v1 on v0

v1 whole, which is shorter than its diff:
```python
import functools

import jax
import jax.numpy as jnp
from jax import lax
from jax.experimental import pallas as pl
from jax.experimental.pallas import tpu as pltpu
from jax.sharding import PartitionSpec as P

DISP = 512
COLS = 128
PAD = 16
WIDE = COLS + PAD
REACH = DISP // COLS
BF16 = jnp.bfloat16
F32 = jnp.float32
VMEM_LIMIT = 48 * 1024 * 1024


def rows_of(refs, image, table, rows):
    return jnp.concatenate([refs[table[row][0]][image, table[row][1]] for row in rows], 0)


def conv_sums(refs, image, table, rows, w_ref, odd, back):
    taps = []
    for col in range(3):
        total = None
        for row in range(3):
            inputs = rows_of(refs, image, table, [r + row - 1 for r in rows])
            if back:
                w_row = jnp.where(odd == 1, row, 2 - row)
                weights = w_ref[w_row * 3 + (2 - col)]
                dims = (((1,), (1,)), ((), ()))
            else:
                w_row = jnp.where(odd == 1, 2 - row, row)
                weights = w_ref[w_row * 3 + col]
                dims = (((1,), (0,)), ((), ()))
            part = lax.dot_general(inputs, weights, dims, preferred_element_type=F32)
            total = part if total is None else total + part
        taps.append(total)
    results = []
    for index in range(len(rows)):
        low, mid, high = (tap[index * WIDE : (index + 1) * WIDE] for tap in taps)
        low = pltpu.roll(low, 1, 0)
        high = pltpu.roll(high, WIDE - 1, 0)
        results.append((low + mid + high)[:COLS])
    return results


def feature_kernel(table, rows, count, *args):
    odd_ref, refs, w_ref = args[0], args[1 : 1 + count], args[1 + count]
    left_ref, right_ref = args[2 + count :]
    odd = odd_ref[0]
    lefts = conv_sums(refs, 0, table, rows, w_ref, odd, False)
    rights = conv_sums(refs, 1, table, rows, w_ref, odd, False)
    slot = lax.broadcasted_iota(jnp.int32, (PAD, 256), 0)
    for index, row in enumerate(rows):
        array, place = table[row]
        code = refs[array][0, place, COLS:].astype(F32)
        code = jnp.where(slot == 1, code, 0.0)
        left, right = lefts[index], rights[index]
        left_ref[index, :COLS] = left.astype(BF16)
        right_ref[index, :COLS] = right.astype(BF16)
        left_ref[index, COLS:] = jnp.where(slot == 0, right[0:1], code).astype(BF16)
        right_ref[index, COLS:] = jnp.where(slot == 0, left[COLS - 1 : COLS], code).astype(BF16)


def grad_kernel(table, rows, count, *args):
    odd_ref, refs, w_ref = args[0], args[1 : 1 + count], args[1 + count]
    outs = args[2 + count :]
    odd = odd_ref[0]
    for image in range(2):
        results = conv_sums(refs, image, table, rows, w_ref, odd, True)
        for index, row in enumerate(rows):
            outs[image][jnp.where(odd == 1, 3 - row, row)] = results[index].astype(BF16)


def vmem_specs(count):
    return [pl.BlockSpec(memory_space=pltpu.VMEM)] * count


def conv_cost(rows):
    return pl.CostEstimate(
        flops=2 * 2 * rows * WIDE * 2304 * 256, bytes_accessed=2 * 2**20, transcendentals=0
    )


def feature_rows(odd, arrays, table, rows, weights):
    shape = jax.ShapeDtypeStruct((len(rows), WIDE, 256), BF16)
    return pl.pallas_call(
        functools.partial(feature_kernel, table, rows, len(arrays)),
        out_shape=(shape, shape),
        in_specs=[pl.BlockSpec(memory_space=pltpu.SMEM)] + vmem_specs(len(arrays) + 1),
        out_specs=tuple(vmem_specs(2)),
        compiler_params=pltpu.CompilerParams(vmem_limit_bytes=VMEM_LIMIT),
        cost_estimate=conv_cost(len(rows)),
        name="features",
    )(odd, *arrays, weights)


def grad_rows(odd, arrays, table, rows, weights):
    shape = jax.ShapeDtypeStruct((4, COLS, 256), BF16)
    return pl.pallas_call(
        functools.partial(grad_kernel, table, rows, len(arrays)),
        out_shape=(shape, shape),
        in_specs=[pl.BlockSpec(memory_space=pltpu.SMEM)] + vmem_specs(len(arrays) + 1),
        out_specs=tuple(vmem_specs(2)),
        compiler_params=pltpu.CompilerParams(vmem_limit_bytes=VMEM_LIMIT),
        cost_estimate=conv_cost(len(rows)),
        name="grads",
    )(odd, *arrays, weights)


def decoded(code):
    low = code[:, COLS:]
    return code[:, :COLS] * 16.0 + low - 1.0, jnp.where(low > 0.5, 0.5, 0.0)


def upright(row):
    return jnp.swapaxes(jnp.broadcast_to(row, (COLS, COLS)), 0, 1)


def gradient(scores, delta, disparity, half_mask):
    inside = jnp.abs(delta - (DISP / 2 - 0.5)) < DISP / 2
    off = delta - disparity
    target = jnp.exp(off * off * (-1.0 / 8.0))
    return jnp.where(inside, half_mask * (scores * (1.0 / 16.0) - target), 0.0).astype(BF16)


def match_kernel(count, *args):
    inner_ref, left_ref, right_ref = args[:3]
    from_left, from_right = args[3 : 3 + REACH], args[3 + REACH : 3 + 2 * REACH]
    out_ref = args[3 + 2 * REACH]
    inner = inner_ref[0].astype(F32)
    slot = lax.broadcasted_iota(jnp.int32, (PAD, 256), 0)
    place = lax.broadcasted_iota(jnp.int32, (WIDE, COLS), 0)
    place = jnp.where(place == WIDE - 1, -1, jnp.where(place > COLS, -(2**16), place))
    place = place.astype(F32)
    lane = lax.broadcasted_iota(jnp.int32, (WIDE, COLS), 1).astype(F32)
    ahead = place - lane
    nt = (((1,), (1,)), ((), ()))
    nn = (((1,), (0,)), ((), ()))
    for row in range(count):
        codes = [decoded(left_ref[row, COLS:].astype(F32)[1:2])]
        codes += [decoded(ref[row, COLS:].astype(F32)[1:2]) for ref in from_right]
        before = decoded(from_left[0][row, COLS:].astype(F32)[1:2])
        rights = [from_left[k - 1][row, :COLS] for k in range(REACH, 0, -1)]
        rights.append(right_ref[row, :COLS])
        lefts = [left_ref[row, :COLS]] + [ref[row, :COLS] for ref in from_right]
        right_cat = jnp.concatenate(rights, 0)
        left_cat = jnp.concatenate(lefts, 0)
        left_after = from_right[0][row, 0:PAD].astype(F32)[0:1]
        left_before = from_left[0][row, COLS:].astype(F32)[0:1]
        right_after = from_right[0][row, COLS:].astype(F32)[0:1]
        right_before = from_left[0][row, COLS - PAD : COLS].astype(F32)[PAD - 1 : PAD]
        left_side = jnp.where(
            slot == 0, left_after, jnp.where(slot == PAD - 1, left_before, 0.0)
        )
        right_side = jnp.where(
            slot == 0, right_after, jnp.where(slot == PAD - 1, right_before, 0.0)
        )
        left_wide = jnp.concatenate([lefts[0], left_side.astype(BF16)], 0)
        right_wide = jnp.concatenate([rights[-1], right_side.astype(BF16)], 0)
        side = slot[:, :COLS]
        disparities, masks = [], []
        for which, parts in ((0, disparities), (1, masks)):
            main = upright(codes[0][which])
            beside = jnp.where(
                side == 0,
                codes[1][which][:, 0:1],
                jnp.where(side == PAD - 1, before[which][:, COLS - 1 : COLS], 0.0),
            )
            parts.append(jnp.concatenate([main, beside], 0))
        scores = lax.dot_general(left_wide, right_cat, nt, preferred_element_type=F32)
        grads = []
        for block in range(REACH + 1):
            tile = scores[:, block * COLS : (block + 1) * COLS]
            delta = ahead + float((REACH - block) * COLS)
            grads.append(gradient(tile, delta, disparities[0], masks[0]))
        left_grad = lax.dot_general(
            jnp.concatenate(grads, 1), right_cat, nn, preferred_element_type=F32
        )
        single = jnp.sum(left_after * right_after, 1, keepdims=True)
        weight = gradient(single, jnp.zeros_like(single), codes[1][0][:, 0:1], codes[1][1][:, 0:1])
        extra = jnp.where(slot == 0, weight.astype(F32) * right_after, 0.0)
        out_ref[0, row, :COLS] = (left_grad[:COLS] * (1.0 / 16.0)).astype(BF16)
        out_ref[0, row, COLS:] = ((left_grad[COLS:] + extra) * (1.0 / 16.0)).astype(BF16)
        scores = lax.dot_general(right_wide, left_cat, nt, preferred_element_type=F32)
        grads = []
        for block in range(REACH + 1):
            tile = scores[:, block * COLS : (block + 1) * COLS]
            delta = float(block * COLS) - ahead
            grads.append(gradient(tile, delta, codes[block][0], codes[block][1]))
        right_grad = lax.dot_general(
            jnp.concatenate(grads, 1), left_cat, nn, preferred_element_type=F32
        )
        single = jnp.sum(left_before * right_before, 1, keepdims=True)
        weight = gradient(
            single,
            jnp.zeros_like(single),
            before[0][:, COLS - 1 : COLS],
            before[1][:, COLS - 1 : COLS],
        )
        extra = jnp.where(slot == PAD - 1, weight.astype(F32) * left_before, 0.0)
        keep = jnp.where(slot == PAD - 1, inner, 1.0)
        out_ref[1, row, :COLS] = (right_grad[:COLS] * (1.0 / 16.0)).astype(BF16)
        out_ref[1, row, COLS:] = ((right_grad[COLS:] + extra) * (1.0 / 16.0) * keep).astype(BF16)


def match_rows(inner, left, right, from_left, from_right):
    count = left.shape[0]
    return pl.pallas_call(
        functools.partial(match_kernel, count),
        out_shape=jax.ShapeDtypeStruct((2, count, WIDE, 256), BF16),
        in_specs=[pl.BlockSpec(memory_space=pltpu.SMEM)] + vmem_specs(2 + 2 * REACH),
        out_specs=pl.BlockSpec(memory_space=pltpu.VMEM),
        compiler_params=pltpu.CompilerParams(vmem_limit_bytes=VMEM_LIMIT),
        cost_estimate=pl.CostEstimate(
            flops=8 * count * WIDE * 640 * 256,
            bytes_accessed=count * 2**20,
            transcendentals=2 * count * WIDE * 640,
        ),
        name="match",
    )(inner, left, right, *from_left, *from_right)


def shifted(value, steps):
    count = lax.axis_size("col")
    pairs = [(i, i + steps) for i in range(count) if 0 <= i + steps < count]
    return lax.ppermute(value, "col", pairs)


def exchanged(left, right):
    from_left = [shifted(right, step) for step in range(1, REACH + 1)]
    from_right = [shifted(left, -step) for step in range(1, REACH + 1)]
    return from_left, from_right


def shards(left_image, right_image, kernel, valid_mask, disparity):
    bands = lax.axis_size("band")
    odd = lax.axis_index("band") % 2
    odd_arg = odd.astype(jnp.int32).reshape(1)
    inner_arg = (lax.axis_index("col") > 0).astype(jnp.int32).reshape(1)
    weights = kernel.reshape(9, 256, 256)
    far_pairs = [(i, i + 1) for i in range(1, bands - 1, 2)]
    far_pairs += [(target, source) for source, target in far_pairs]
    near_pairs = [(i, i ^ 1) for i in range(bands)]

    stacked = jnp.stack((left_image, right_image), 0)
    own = jnp.where(odd == 1, stacked[:, ::-1], stacked)
    code = jnp.concatenate(
        [disparity >> 4, jnp.where(valid_mask > 0, (disparity & 15) + 1, 0)], 1
    ).astype(BF16)
    code = jnp.where(odd == 1, code[::-1], code)

    low = shifted(own[:, :, COLS - 1 :], 1)
    high = shifted(own[:, :, :1], -1)
    code = jnp.broadcast_to(code[None, :, None], (2, 4, 1, 256))
    blank = jnp.zeros((2, 4, PAD - 3, 256), BF16)
    own = jnp.concatenate([own, high, code, blank, low], 2)

    far = lax.ppermute(own[:, :2], "band", far_pairs)
    near = lax.ppermute(own[:, 3:], "band", near_pairs)

    table = {row: (0, row) for row in range(4)}
    left, right = feature_rows(
        odd_arg, (own, near), {**table, 4: (1, 0)}, (1, 2, 3), weights
    )
    inside = match_rows(inner_arg, left, right, *exchanged(left, right))
    near_grad = lax.ppermute(inside[:, 2:], "band", near_pairs)

    left, right = feature_rows(
        odd_arg, (own, far), {**table, -1: (1, 0), -2: (1, 1)}, (-1, 0), weights
    )
    edge = match_rows(inner_arg, left, right, *exchanged(left, right))

    grads = {-1: (0, 0), 0: (0, 1), 1: (1, 0), 2: (1, 1), 3: (1, 2), 4: (2, 0)}
    return grad_rows(odd_arg, (edge, inside, near_grad), grads, (0, 1, 2, 3), weights)


def solution(mesh):
    return jax.shard_map(
        shards,
        mesh=mesh,
        in_specs=(
            P("band", "col", None),
            P("band", "col", None),
            P(),
            P("band", "col"),
            P("band", "col"),
        ),
        out_specs=(P("band", "col", None), P("band", "col", None)),
        check_vma=False,
    )
```

time: 150 us -> 115 us (0.77)
  the two profiles are of different devices: /device:TPU:5 before, /device:TPU:2 now
where the time goes in v1:
time: 115 us; the launch traced here: 114 us
  starting transfers between devices  89.7 us (78%)
  waiting for transfers between devices  14.8 us (13%)
  Pallas kernels  6.91 us (6%)
  other arithmetic  1.2 us (1%)
    ppermute x18, starting transfers between devices, shifted(): return lax.ppermute(value, 'col', pairs)  69.9 us
    ppermute x1, starting transfers between devices, shards(): far = lax.ppermute(own[:, :2], 'band', far_pairs)  15.8 us
    ppermute x18, waiting for transfers between devices, shifted(): return lax.ppermute(value, 'col', pairs)  14.8 us
    pallas_call x2, Pallas kernels, match_rows(): pl.pallas_call(functools.partial(match_kernel, count), out_shape=jax.Shap...  2.56 us
  transfers between devices with their start and end apart: 21, of which 6 were waited for; matrix products, arithmetic and copies ran while one was open for 0% of the time, Pallas kernels for 4%

profile of v1, /device:TPU:2, one launch (start us, length us, event | category | flops | bytes accessed | tf_op | source)
XLA Modules:
  0.0 114.3 jit_solution(612166116609522202)
XLA Ops:
  0.6 0.0 copy-start.3
  0.6 0.0 copy-start.4
  0.7 1.1 pad_maximum_fusion
  1.7 0.1 reverse_select_fusion
  1.9 0.0 copy-start
  1.9 1.4 %collective-permute-start = (bf16[2,4,1,256]{3,2,1,0:T(2,128)(2,1)S(1)}, bf16[2,4,1,256]{3,2,1,0:T(2,128)(2,1)S(1)}, u32[]{:S(2)}, u32[]{:S(2)}) collective-permute-start(bf16[2,4,1,256]{3,2,1,0:T(2,128)(2,1)S(1)} %get-tuple-element.11), channel_id=1, source_target_pairs={{1,0},{2,1},{3,2},{4,3},{5,4},{6,5},{7,6},{8,7},{9,8},{10,9},{11,1... | collective-permute-start | bytes 12296 | tf_op jit(solution)/shard_map/ppermute | solution.py:230
  3.3 4.5 %collective-permute-start.1 = (bf16[2,4,1,256]{3,2,1,0:T(2,128)(2,1)S(1)}, bf16[2,4,1,256]{3,2,1,0:T(2,128)(2,1)S(1)}, u32[]{:S(2)}, u32[]{:S(2)}) collective-permute-start(bf16[2,4,1,256]{3,2,1,0:T(2,128)(2,1)S(1)} %get-tuple-element.10), channel_id=1, source_target_pairs={{0,1},{1,2},{2,3},{3,4},{4,5},{5,6},{6,7},{7,8},{8,9},{9,10},{10,1... | collective-permute-start | bytes 12296 | tf_op jit(solution)/shard_map/ppermute | solution.py:230
  7.9 0.0 copy-done.3
  7.9 0.0 copy-done.4
  7.9 0.1 rev.7
  8.0 0.0 collective-permute-done
  8.0 1.2 %collective-permute-done.1 = bf16[2,4,1,256]{3,2,1,0:T(2,128)(2,1)S(1)} collective-permute-done((bf16[2,4,1,256]{3,2,1,0:T(2,128)(2,1)S(1)}, bf16[2,4,1,256]{3,2,1,0:T(2,128)(2,1)S(1)}, u32[]{:S(2)}, u32[]{:S(2)}) %collective-permute-start.1) | collective-permute-done | bytes 4128 | tf_op jit(solution)/shard_map/ppermute | solution.py:230
  9.2 0.4 concatenate.8.args_1_
  9.7 1.9 %collective-permute-start.11 = (bf16[2,1,144,256]{3,2,1,0:T(8,128)(2,1)S(1)}, bf16[2,1,144,256]{3,2,1,0:T(8,128)(2,1)S(1)}, u32[]{:S(2)}, u32[]{:S(2)}) collective-permute-start(bf16[2,1,144,256]{3,2,1,0:T(8,128)(2,1)S(1)} %slice.23), channel_id=1, source_target_pairs={{0,32},{32,0},{64,96},{96,64},{128,160},{160,128},{192,224},{224,1... | collective-permute-start | bytes 442376 | tf_op jit(solution)/shard_map/ppermute | solution.py:263
  11.6 15.8 %collective-permute-start.2 = (bf16[2,2,144,256]{3,2,1,0:T(8,128)(2,1)S(1)}, bf16[2,2,144,256]{3,2,1,0:T(8,128)(2,1)S(1)}, u32[]{:S(2)}, u32[]{:S(2)}) collective-permute-start(bf16[2,2,144,256]{3,2,1,0:T(8,128)(2,1)S(1)} %slice.22), channel_id=1, source_target_pairs={{32,64},{96,128},{160,192},{224,256},{288,320},{352,384},{416,448}... | collective-permute-start | bytes 884744 | tf_op jit(solution)/shard_map/ppermute | solution.py:262
  27.4 0.0 collective-permute-done.11.args_2_
  27.5 0.0 copy-done
  27.5 0.0 copy-start.1
  27.5 1.2 %features.3 = (bf16[3,144,256]{2,1,0:T(8,128)(2,1)S(1)}, bf16[3,144,256]{2,1,0:T(8,128)(2,1)S(1)}) custom-call(s32[1]{0:T(128)} %bitcast.args_0_, bf16[2,4,144,256]{3,2,1,0:T(8,128)(2,1)S(1)} %concatenate.8.args_1_, bf16[2,1,144,256]{3,2,1,0:T(8,128)(2,1)S(1)} %collective-permute-done.11.args_2_, bf16[9,256,256]{2,1,0:T(8,128)(2,1)S(1)} %bitcast.5), custom_call_target="tpu_custom_call" | custom-call | flops 1019215872 | bytes 2097152 | tf_op jit(solution)/shard_map/features/pallas_call | solution.py:90
  28.7 4.2 %collective-permute-start.12 = (bf16[3,144,256]{2,1,0:T(8,128)(2,1)S(1)}, bf16[3,144,256]{2,1,0:T(8,128)(2,1)S(1)}, u32[]{:S(2)}, u32[]{:S(2)}) collective-permute-start(bf16[3,144,256]{2,1,0:T(8,128)(2,1)S(1)} %get-tuple-element.9.args_2_), channel_id=1, source_target_pairs={{0,1},{1,2},{2,3},{3,4},{4,5},{5,6},{6,7},{7,8},{8,9},{9,10},{10,1... | collective-permute-start | bytes 663560 | tf_op jit(solution)/shard_map/ppermute | solution.py:230
  32.9 6.2 %collective-permute-start.13 = (bf16[3,144,256]{2,1,0:T(8,128)(2,1)S(1)}, bf16[3,144,256]{2,1,0:T(8,128)(2,1)S(1)}, u32[]{:S(2)}, u32[]{:S(2)}) collective-permute-start(bf16[3,144,256]{2,1,0:T(8,128)(2,1)S(1)} %get-tuple-element.9.args_2_), channel_id=1, source_target_pairs={{0,2},{1,3},{2,4},{3,5},{4,6},{5,7},{6,8},{7,9},{8,10},{9,11},{10,... | collective-permute-start | bytes 663560 | tf_op jit(solution)/shard_map/ppermute | solution.py:230
  39.1 4.9 %collective-permute-start.14 = (bf16[3,144,256]{2,1,0:T(8,128)(2,1)S(1)}, bf16[3,144,256]{2,1,0:T(8,128)(2,1)S(1)}, u32[]{:S(2)}, u32[]{:S(2)}) collective-permute-start(bf16[3,144,256]{2,1,0:T(8,128)(2,1)S(1)} %get-tuple-element.9.args_2_), channel_id=1, source_target_pairs={{0,3},{1,4},{2,5},{3,6},{4,7},{5,8},{6,9},{7,10},{8,11},{9,12},{10... | collective-permute-start | bytes 663560 | tf_op jit(solution)/shard_map/ppermute | solution.py:230
  44.0 2.9 %collective-permute-start.15 = (bf16[3,144,256]{2,1,0:T(8,128)(2,1)S(1)}, bf16[3,144,256]{2,1,0:T(8,128)(2,1)S(1)}, u32[]{:S(2)}, u32[]{:S(2)}) collective-permute-start(bf16[3,144,256]{2,1,0:T(8,128)(2,1)S(1)} %get-tuple-element.9.args_2_), channel_id=1, source_target_pairs={{0,4},{1,5},{2,6},{3,7},{4,8},{5,9},{6,10},{7,11},{8,12},{9,13},{1... | collective-permute-start | bytes 663560 | tf_op jit(solution)/shard_map/ppermute | solution.py:230
  46.9 0.0 collective-permute-done.2.args_2_
  46.9 1.3 %collective-permute-start.16 = (bf16[3,144,256]{2,1,0:T(8,128)(2,1)S(1)}, bf16[3,144,256]{2,1,0:T(8,128)(2,1)S(1)}, u32[]{:S(2)}, u32[]{:S(2)}) collective-permute-start(bf16[3,144,256]{2,1,0:T(8,128)(2,1)S(1)} %get-tuple-element.8.args_1_), channel_id=1, source_target_pairs={{1,0},{2,1},{3,2},{4,3},{5,4},{6,5},{7,6},{8,7},{9,8},{10,9},{11,1... | collective-permute-start | bytes 663560 | tf_op jit(solution)/shard_map/ppermute | solution.py:230
  48.2 0.0 collective-permute-done.12.args_3_
  48.2 1.3 %collective-permute-start.17 = (bf16[3,144,256]{2,1,0:T(8,128)(2,1)S(1)}, bf16[3,144,256]{2,1,0:T(8,128)(2,1)S(1)}, u32[]{:S(2)}, u32[]{:S(2)}) collective-permute-start(bf16[3,144,256]{2,1,0:T(8,128)(2,1)S(1)} %get-tuple-element.8.args_1_), channel_id=1, source_target_pairs={{2,0},{3,1},{4,2},{5,3},{6,4},{7,5},{8,6},{9,7},{10,8},{11,9},{12,... | collective-permute-start | bytes 663560 | tf_op jit(solution)/shard_map/ppermute | solution.py:230
  49.5 0.0 collective-permute-done.13.args_4_
  49.5 1.3 %collective-permute-start.18 = (bf16[3,144,256]{2,1,0:T(8,128)(2,1)S(1)}, bf16[3,144,256]{2,1,0:T(8,128)(2,1)S(1)}, u32[]{:S(2)}, u32[]{:S(2)}) collective-permute-start(bf16[3,144,256]{2,1,0:T(8,128)(2,1)S(1)} %get-tuple-element.8.args_1_), channel_id=1, source_target_pairs={{3,0},{4,1},{5,2},{6,3},{7,4},{8,5},{9,6},{10,7},{11,8},{12,9},{13... | collective-permute-start | bytes 663560 | tf_op jit(solution)/shard_map/ppermute | solution.py:230
  50.8 0.8 collective-permute-done.14.args_5_
  51.7 1.3 %collective-permute-start.19 = (bf16[3,144,256]{2,1,0:T(8,128)(2,1)S(1)}, bf16[3,144,256]{2,1,0:T(8,128)(2,1)S(1)}, u32[]{:S(2)}, u32[]{:S(2)}) collective-permute-start(bf16[3,144,256]{2,1,0:T(8,128)(2,1)S(1)} %get-tuple-element.8.args_1_), channel_id=1, source_target_pairs={{4,0},{5,1},{6,2},{7,3},{8,4},{9,5},{10,6},{11,7},{12,8},{13,9},{1... | collective-permute-start | bytes 663560 | tf_op jit(solution)/shard_map/ppermute | solution.py:230
  53.0 0.0 copy-done.1
  53.0 0.9 features.2
  53.8 4.1 %collective-permute-done.15.args_6_ = bf16[3,144,256]{2,1,0:T(8,128)(2,1)S(1)} collective-permute-done((bf16[3,144,256]{2,1,0:T(8,128)(2,1)S(1)}, bf16[3,144,256]{2,1,0:T(8,128)(2,1)S(1)}, u32[]{:S(2)}, u32[]{:S(2)}) %collective-permute-start.15) | collective-permute-done | bytes 221216 | tf_op jit(solution)/shard_map/ppermute | solution.py:230
  58.0 8.6 %collective-permute-start.3 = (bf16[2,144,256]{2,1,0:T(8,128)(2,1)S(1)}, bf16[2,144,256]{2,1,0:T(8,128)(2,1)S(1)}, u32[]{:S(2)}, u32[]{:S(2)}) collective-permute-start(bf16[2,144,256]{2,1,0:T(8,128)(2,1)S(1)} %get-tuple-element.7.args_2_), channel_id=1, source_target_pairs={{0,1},{1,2},{2,3},{3,4},{4,5},{5,6},{6,7},{7,8},{8,9},{9,10},{10,1... | collective-permute-start | bytes 442376 | tf_op jit(solution)/shard_map/ppermute | solution.py:230
  66.6 0.0 collective-permute-done.16.args_7_
  66.6 18.7 %collective-permute-start.4 = (bf16[2,144,256]{2,1,0:T(8,128)(2,1)S(1)}, bf16[2,144,256]{2,1,0:T(8,128)(2,1)S(1)}, u32[]{:S(2)}, u32[]{:S(2)}) collective-permute-start(bf16[2,144,256]{2,1,0:T(8,128)(2,1)S(1)} %get-tuple-element.7.args_2_), channel_id=1, source_target_pairs={{0,2},{1,3},{2,4},{3,5},{4,6},{5,7},{6,8},{7,9},{8,10},{9,11},{10,... | collective-permute-start | bytes 442376 | tf_op jit(solution)/shard_map/ppermute | solution.py:230
  85.3 0.0 collective-permute-done.17.args_8_
  85.3 4.1 %collective-permute-start.5 = (bf16[2,144,256]{2,1,0:T(8,128)(2,1)S(1)}, bf16[2,144,256]{2,1,0:T(8,128)(2,1)S(1)}, u32[]{:S(2)}, u32[]{:S(2)}) collective-permute-start(bf16[2,144,256]{2,1,0:T(8,128)(2,1)S(1)} %get-tuple-element.7.args_2_), channel_id=1, source_target_pairs={{0,3},{1,4},{2,5},{3,6},{4,7},{5,8},{6,9},{7,10},{8,11},{9,12},{10... | collective-permute-start | bytes 442376 | tf_op jit(solution)/shard_map/ppermute | solution.py:230
  89.5 0.0 collective-permute-done.18.args_9_
  89.5 3.9 %collective-permute-start.6 = (bf16[2,144,256]{2,1,0:T(8,128)(2,1)S(1)}, bf16[2,144,256]{2,1,0:T(8,128)(2,1)S(1)}, u32[]{:S(2)}, u32[]{:S(2)}) collective-permute-start(bf16[2,144,256]{2,1,0:T(8,128)(2,1)S(1)} %get-tuple-element.7.args_2_), channel_id=1, source_target_pairs={{0,4},{1,5},{2,6},{3,7},{4,8},{5,9},{6,10},{7,11},{8,12},{9,13},{1... | collective-permute-start | bytes 442376 | tf_op jit(solution)/shard_map/ppermute | solution.py:230
  93.4 0.0 collective-permute-done.19.args_10_
  93.4 1.3 %collective-permute-start.7 = (bf16[2,144,256]{2,1,0:T(8,128)(2,1)S(1)}, bf16[2,144,256]{2,1,0:T(8,128)(2,1)S(1)}, u32[]{:S(2)}, u32[]{:S(2)}) collective-permute-start(bf16[2,144,256]{2,1,0:T(8,128)(2,1)S(1)} %get-tuple-element.6.args_1_), channel_id=1, source_target_pairs={{1,0},{2,1},{3,2},{4,3},{5,4},{6,5},{7,6},{8,7},{9,8},{10,9},{11,1... | collective-permute-start | bytes 442376 | tf_op jit(solution)/shard_map/ppermute | solution.py:230
  94.7 0.0 collective-permute-done.3.args_3_
  94.8 1.3 %collective-permute-start.8 = (bf16[2,144,256]{2,1,0:T(8,128)(2,1)S(1)}, bf16[2,144,256]{2,1,0:T(8,128)(2,1)S(1)}, u32[]{:S(2)}, u32[]{:S(2)}) collective-permute-start(bf16[2,144,256]{2,1,0:T(8,128)(2,1)S(1)} %get-tuple-element.6.args_1_), channel_id=1, source_target_pairs={{2,0},{3,1},{4,2},{5,3},{6,4},{7,5},{8,6},{9,7},{10,8},{11,9},{12,... | collective-permute-start | bytes 442376 | tf_op jit(solution)/shard_map/ppermute | solution.py:230
  96.1 0.0 collective-permute-done.4.args_4_
  96.1 1.3 %collective-permute-start.9 = (bf16[2,144,256]{2,1,0:T(8,128)(2,1)S(1)}, bf16[2,144,256]{2,1,0:T(8,128)(2,1)S(1)}, u32[]{:S(2)}, u32[]{:S(2)}) collective-permute-start(bf16[2,144,256]{2,1,0:T(8,128)(2,1)S(1)} %get-tuple-element.6.args_1_), channel_id=1, source_target_pairs={{3,0},{4,1},{5,2},{6,3},{7,4},{8,5},{9,6},{10,7},{11,8},{12,9},{13... | collective-permute-start | bytes 442376 | tf_op jit(solution)/shard_map/ppermute | solution.py:230
  97.4 0.0 collective-permute-done.5.args_5_
  97.4 1.3 %collective-permute-start.10 = (bf16[2,144,256]{2,1,0:T(8,128)(2,1)S(1)}, bf16[2,144,256]{2,1,0:T(8,128)(2,1)S(1)}, u32[]{:S(2)}, u32[]{:S(2)}) collective-permute-start(bf16[2,144,256]{2,1,0:T(8,128)(2,1)S(1)} %get-tuple-element.6.args_1_), channel_id=1, source_target_pairs={{4,0},{5,1},{6,2},{7,3},{8,4},{9,5},{10,6},{11,7},{12,8},{13,9},{1... | collective-permute-start | bytes 442376 | tf_op jit(solution)/shard_map/ppermute | solution.py:230
  98.7 1.5 %match.3.args_2_ = bf16[2,3,144,256]{3,2,1,0:T(8,128)(2,1)S(1)} custom-call(s32[1]{0:T(128)} %bitcast.1.args_0_, bf16[3,144,256]{2,1,0:T(8,128)(2,1)S(1)} %get-tuple-element.8.args_1_, bf16[3,144,256]{2,1,0:T(8,128)(2,1)S(1)} %get-tuple-element.9.args_2_, bf16[3,144,256]{2,1,0:T(8,128)(2,1)S(1)} %collective-permute-done.12.args_3_, ...), custom_call_target="tpu_custom_call" | custom-call | flops 566231040 | bytes 3145728 | tf_op jit(solution)/shard_map/match/pallas_call | solution.py:212
  100.2 0.0 copy-start.2
  100.2 0.0 collective-permute-done.6.args_6_
  100.2 2.1 %collective-permute-start.20 = (bf16[2,1,144,256]{3,2,1,0:T(8,128)(2,1)S(1)}, bf16[2,1,144,256]{3,2,1,0:T(8,128)(2,1)S(1)}, u32[]{:S(2)}, u32[]{:S(2)}) collective-permute-start(bf16[2,1,144,256]{3,2,1,0:T(8,128)(2,1)S(1)} %slice.24), channel_id=1, source_target_pairs={{0,32},{32,0},{64,96},{96,64},{128,160},{160,128},{192,224},{224,1... | collective-permute-start | bytes 442376 | tf_op jit(solution)/shard_map/ppermute | solution.py:270
  102.3 0.0 collective-permute-done.7.args_7_
  102.3 1.4 %collective-permute-done.8.args_8_ = bf16[2,144,256]{2,1,0:T(8,128)(2,1)S(1)} collective-permute-done((bf16[2,144,256]{2,1,0:T(8,128)(2,1)S(1)}, bf16[2,144,256]{2,1,0:T(8,128)(2,1)S(1)}, u32[]{:S(2)}, u32[]{:S(2)}) %collective-permute-start.8) | collective-permute-done | bytes 147488 | tf_op jit(solution)/shard_map/ppermute | solution.py:230
  103.6 3.4 %collective-permute-done.9.args_9_ = bf16[2,144,256]{2,1,0:T(8,128)(2,1)S(1)} collective-permute-done((bf16[2,144,256]{2,1,0:T(8,128)(2,1)S(1)}, bf16[2,144,256]{2,1,0:T(8,128)(2,1)S(1)}, u32[]{:S(2)}, u32[]{:S(2)}) %collective-permute-start.9) | collective-permute-done | bytes 147488 | tf_op jit(solution)/shard_map/ppermute | solution.py:230
  107.0 3.9 %collective-permute-done.10.args_10_ = bf16[2,144,256]{2,1,0:T(8,128)(2,1)S(1)} collective-permute-done((bf16[2,144,256]{2,1,0:T(8,128)(2,1)S(1)}, bf16[2,144,256]{2,1,0:T(8,128)(2,1)S(1)}, u32[]{:S(2)}, u32[]{:S(2)}) %collective-permute-start.10) | collective-permute-done | bytes 147488 | tf_op jit(solution)/shard_map/ppermute | solution.py:230
  110.9 1.1 match.2.args_1_
  112.0 0.0 collective-permute-done.20.args_3_
  112.0 0.0 copy-done.2
  112.0 2.3 %grads.1 = (bf16[4,128,256]{2,1,0:T(8,128)(2,1)}, bf16[4,128,256]{2,1,0:T(8,128)(2,1)}) custom-call(s32[1]{0:T(128)} %bitcast.args_0_, bf16[2,2,144,256]{3,2,1,0:T(8,128)(2,1)S(1)} %match.2.args_1_, bf16[2,3,144,256]{3,2,1,0:T(8,128)(2,1)S(1)} %match.3.args_2_, bf16[2,1,144,256]{3,2,1,0:T(8,128)(2,1)S(1)} %collective-permute-done.20.args_3_, ...), custom_call_target="tpu_custom_call" | custom-call | flops 1358954496 | bytes 2097152 | tf_op jit(solution)/shard_map/grads/pallas_call | solution.py:103
  (9 shorter events, 0.1 us)
Async XLA Ops:
  0.6 7.3 %copy-start.3 = (s32[4,128]{1,0:T(4,128)S(1)}, s32[4,128]{1,0:T(4,128)}, u32[]{:S(2)}) copy-start(s32[4,128]{1,0:T(4,128)} %param.9) | copy-start | bytes 6148
  0.6 7.3 %copy-start.4 = (s32[4,128]{1,0:T(4,128)S(1)}, s32[4,128]{1,0:T(4,128)}, u32[]{:S(2)}) copy-start(s32[4,128]{1,0:T(4,128)} %param.8) | copy-start | bytes 6148
  1.9 25.6 %copy-start = (bf16[2304,256]{1,0:T(8,128)(2,1)S(1)}, bf16[2304,256]{1,0:T(8,128)(2,1)}, u32[]{:S(2)}) copy-start(bf16[2304,256]{1,0:T(8,128)(2,1)} %param.7) | copy-start | bytes 3538948
  1.9 6.1 %collective-permute-start = (bf16[2,4,1,256]{3,2,1,0:T(2,128)(2,1)S(1)}, bf16[2,4,1,256]{3,2,1,0:T(2,128)(2,1)S(1)}, u32[]{:S(2)}, u32[]{:S(2)}) collective-permute-start(bf16[2,4,1,256]{3,2,1,0:T(2,128)(2,1)S(1)} %get-tuple-element.11), channel_id=1, source_target_pairs={{1,0},{2,1},{3,2},{4,3},{5,4},{6,5},{7,6},{8,7},{9,8},{10,9},{11,1... | collective-permute-start | bytes 12296 | tf_op jit(solution)/shard_map/ppermute | solution.py:230
  3.3 5.9 %collective-permute-start.1 = (bf16[2,4,1,256]{3,2,1,0:T(2,128)(2,1)S(1)}, bf16[2,4,1,256]{3,2,1,0:T(2,128)(2,1)S(1)}, u32[]{:S(2)}, u32[]{:S(2)}) collective-permute-start(bf16[2,4,1,256]{3,2,1,0:T(2,128)(2,1)S(1)} %get-tuple-element.10), channel_id=1, source_target_pairs={{0,1},{1,2},{2,3},{3,4},{4,5},{5,6},{6,7},{7,8},{8,9},{9,10},{10,1... | collective-permute-start | bytes 12296 | tf_op jit(solution)/shard_map/ppermute | solution.py:230
  9.7 17.8 %collective-permute-start.11 = (bf16[2,1,144,256]{3,2,1,0:T(8,128)(2,1)S(1)}, bf16[2,1,144,256]{3,2,1,0:T(8,128)(2,1)S(1)}, u32[]{:S(2)}, u32[]{:S(2)}) collective-permute-start(bf16[2,1,144,256]{3,2,1,0:T(8,128)(2,1)S(1)} %slice.23), channel_id=1, source_target_pairs={{0,32},{32,0},{64,96},{96,64},{128,160},{160,128},{192,224},{224,1... | collective-permute-start | bytes 442376 | tf_op jit(solution)/shard_map/ppermute | solution.py:263
  11.6 35.3 %collective-permute-start.2 = (bf16[2,2,144,256]{3,2,1,0:T(8,128)(2,1)S(1)}, bf16[2,2,144,256]{3,2,1,0:T(8,128)(2,1)S(1)}, u32[]{:S(2)}, u32[]{:S(2)}) collective-permute-start(bf16[2,2,144,256]{3,2,1,0:T(8,128)(2,1)S(1)} %slice.22), channel_id=1, source_target_pairs={{32,64},{96,128},{160,192},{224,256},{288,320},{352,384},{416,448}... | collective-permute-start | bytes 884744 | tf_op jit(solution)/shard_map/ppermute | solution.py:262
  27.5 25.5 %copy-start.1 = (bf16[2304,256]{1,0:T(8,128)(2,1)S(1)}, bf16[2304,256]{1,0:T(8,128)(2,1)}, u32[]{:S(2)}) copy-start(bf16[2304,256]{1,0:T(8,128)(2,1)} %param.7) | copy-start | bytes 3538948
  28.7 19.5 %collective-permute-start.12 = (bf16[3,144,256]{2,1,0:T(8,128)(2,1)S(1)}, bf16[3,144,256]{2,1,0:T(8,128)(2,1)S(1)}, u32[]{:S(2)}, u32[]{:S(2)}) collective-permute-start(bf16[3,144,256]{2,1,0:T(8,128)(2,1)S(1)} %get-tuple-element.9.args_2_), channel_id=1, source_target_pairs={{0,1},{1,2},{2,3},{3,4},{4,5},{5,6},{6,7},{7,8},{8,9},{9,10},{10,1... | collective-permute-start | bytes 663560 | tf_op jit(solution)/shard_map/ppermute | solution.py:230
  32.9 16.6 %collective-permute-start.13 = (bf16[3,144,256]{2,1,0:T(8,128)(2,1)S(1)}, bf16[3,144,256]{2,1,0:T(8,128)(2,1)S(1)}, u32[]{:S(2)}, u32[]{:S(2)}) collective-permute-start(bf16[3,144,256]{2,1,0:T(8,128)(2,1)S(1)} %get-tuple-element.9.args_2_), channel_id=1, source_target_pairs={{0,2},{1,3},{2,4},{3,5},{4,6},{5,7},{6,8},{7,9},{8,10},{9,11},{10,... | collective-permute-start | bytes 663560 | tf_op jit(solution)/shard_map/ppermute | solution.py:230
  39.1 12.5 %collective-permute-start.14 = (bf16[3,144,256]{2,1,0:T(8,128)(2,1)S(1)}, bf16[3,144,256]{2,1,0:T(8,128)(2,1)S(1)}, u32[]{:S(2)}, u32[]{:S(2)}) collective-permute-start(bf16[3,144,256]{2,1,0:T(8,128)(2,1)S(1)} %get-tuple-element.9.args_2_), channel_id=1, source_target_pairs={{0,3},{1,4},{2,5},{3,6},{4,7},{5,8},{6,9},{7,10},{8,11},{9,12},{10... | collective-permute-start | bytes 663560 | tf_op jit(solution)/shard_map/ppermute | solution.py:230
  44.0 14.0 %collective-permute-start.15 = (bf16[3,144,256]{2,1,0:T(8,128)(2,1)S(1)}, bf16[3,144,256]{2,1,0:T(8,128)(2,1)S(1)}, u32[]{:S(2)}, u32[]{:S(2)}) collective-permute-start(bf16[3,144,256]{2,1,0:T(8,128)(2,1)S(1)} %get-tuple-element.9.args_2_), channel_id=1, source_target_pairs={{0,4},{1,5},{2,6},{3,7},{4,8},{5,9},{6,10},{7,11},{8,12},{9,13},{1... | collective-permute-start | bytes 663560 | tf_op jit(solution)/shard_map/ppermute | solution.py:230
  46.9 19.6 %collective-permute-start.16 = (bf16[3,144,256]{2,1,0:T(8,128)(2,1)S(1)}, bf16[3,144,256]{2,1,0:T(8,128)(2,1)S(1)}, u32[]{:S(2)}, u32[]{:S(2)}) collective-permute-start(bf16[3,144,256]{2,1,0:T(8,128)(2,1)S(1)} %get-tuple-element.8.args_1_), channel_id=1, source_target_pairs={{1,0},{2,1},{3,2},{4,3},{5,4},{6,5},{7,6},{8,7},{9,8},{10,9},{11,1... | collective-permute-start | bytes 663560 | tf_op jit(solution)/shard_map/ppermute | solution.py:230
  48.2 37.1 %collective-permute-start.17 = (bf16[3,144,256]{2,1,0:T(8,128)(2,1)S(1)}, bf16[3,144,256]{2,1,0:T(8,128)(2,1)S(1)}, u32[]{:S(2)}, u32[]{:S(2)}) collective-permute-start(bf16[3,144,256]{2,1,0:T(8,128)(2,1)S(1)} %get-tuple-element.8.args_1_), channel_id=1, source_target_pairs={{2,0},{3,1},{4,2},{5,3},{6,4},{7,5},{8,6},{9,7},{10,8},{11,9},{12,... | collective-permute-start | bytes 663560 | tf_op jit(solution)/shard_map/ppermute | solution.py:230
  49.5 39.9 %collective-permute-start.18 = (bf16[3,144,256]{2,1,0:T(8,128)(2,1)S(1)}, bf16[3,144,256]{2,1,0:T(8,128)(2,1)S(1)}, u32[]{:S(2)}, u32[]{:S(2)}) collective-permute-start(bf16[3,144,256]{2,1,0:T(8,128)(2,1)S(1)} %get-tuple-element.8.args_1_), channel_id=1, source_target_pairs={{3,0},{4,1},{5,2},{6,3},{7,4},{8,5},{9,6},{10,7},{11,8},{12,9},{13... | collective-permute-start | bytes 663560 | tf_op jit(solution)/shard_map/ppermute | solution.py:230
  51.7 41.8 %collective-permute-start.19 = (bf16[3,144,256]{2,1,0:T(8,128)(2,1)S(1)}, bf16[3,144,256]{2,1,0:T(8,128)(2,1)S(1)}, u32[]{:S(2)}, u32[]{:S(2)}) collective-permute-start(bf16[3,144,256]{2,1,0:T(8,128)(2,1)S(1)} %get-tuple-element.8.args_1_), channel_id=1, source_target_pairs={{4,0},{5,1},{6,2},{7,3},{8,4},{9,5},{10,6},{11,7},{12,8},{13,9},{1... | collective-permute-start | bytes 663560 | tf_op jit(solution)/shard_map/ppermute | solution.py:230
  58.0 36.8 %collective-permute-start.3 = (bf16[2,144,256]{2,1,0:T(8,128)(2,1)S(1)}, bf16[2,144,256]{2,1,0:T(8,128)(2,1)S(1)}, u32[]{:S(2)}, u32[]{:S(2)}) collective-permute-start(bf16[2,144,256]{2,1,0:T(8,128)(2,1)S(1)} %get-tuple-element.7.args_2_), channel_id=1, source_target_pairs={{0,1},{1,2},{2,3},{3,4},{4,5},{5,6},{6,7},{7,8},{8,9},{9,10},{10,1... | collective-permute-start | bytes 442376 | tf_op jit(solution)/shard_map/ppermute | solution.py:230
  66.6 29.5 %collective-permute-start.4 = (bf16[2,144,256]{2,1,0:T(8,128)(2,1)S(1)}, bf16[2,144,256]{2,1,0:T(8,128)(2,1)S(1)}, u32[]{:S(2)}, u32[]{:S(2)}) collective-permute-start(bf16[2,144,256]{2,1,0:T(8,128)(2,1)S(1)} %get-tuple-element.7.args_2_), channel_id=1, source_target_pairs={{0,2},{1,3},{2,4},{3,5},{4,6},{5,7},{6,8},{7,9},{8,10},{9,11},{10,... | collective-permute-start | bytes 442376 | tf_op jit(solution)/shard_map/ppermute | solution.py:230
  85.3 12.0 %collective-permute-start.5 = (bf16[2,144,256]{2,1,0:T(8,128)(2,1)S(1)}, bf16[2,144,256]{2,1,0:T(8,128)(2,1)S(1)}, u32[]{:S(2)}, u32[]{:S(2)}) collective-permute-start(bf16[2,144,256]{2,1,0:T(8,128)(2,1)S(1)} %get-tuple-element.7.args_2_), channel_id=1, source_target_pairs={{0,3},{1,4},{2,5},{3,6},{4,7},{5,8},{6,9},{7,10},{8,11},{9,12},{10... | collective-permute-start | bytes 442376 | tf_op jit(solution)/shard_map/ppermute | solution.py:230
  89.5 10.7 %collective-permute-start.6 = (bf16[2,144,256]{2,1,0:T(8,128)(2,1)S(1)}, bf16[2,144,256]{2,1,0:T(8,128)(2,1)S(1)}, u32[]{:S(2)}, u32[]{:S(2)}) collective-permute-start(bf16[2,144,256]{2,1,0:T(8,128)(2,1)S(1)} %get-tuple-element.7.args_2_), channel_id=1, source_target_pairs={{0,4},{1,5},{2,6},{3,7},{4,8},{5,9},{6,10},{7,11},{8,12},{9,13},{1... | collective-permute-start | bytes 442376 | tf_op jit(solution)/shard_map/ppermute | solution.py:230
  93.4 8.8 %collective-permute-start.7 = (bf16[2,144,256]{2,1,0:T(8,128)(2,1)S(1)}, bf16[2,144,256]{2,1,0:T(8,128)(2,1)S(1)}, u32[]{:S(2)}, u32[]{:S(2)}) collective-permute-start(bf16[2,144,256]{2,1,0:T(8,128)(2,1)S(1)} %get-tuple-element.6.args_1_), channel_id=1, source_target_pairs={{1,0},{2,1},{3,2},{4,3},{5,4},{6,5},{7,6},{8,7},{9,8},{10,9},{11,1... | collective-permute-start | bytes 442376 | tf_op jit(solution)/shard_map/ppermute | solution.py:230
  94.8 8.9 %collective-permute-start.8 = (bf16[2,144,256]{2,1,0:T(8,128)(2,1)S(1)}, bf16[2,144,256]{2,1,0:T(8,128)(2,1)S(1)}, u32[]{:S(2)}, u32[]{:S(2)}) collective-permute-start(bf16[2,144,256]{2,1,0:T(8,128)(2,1)S(1)} %get-tuple-element.6.args_1_), channel_id=1, source_target_pairs={{2,0},{3,1},{4,2},{5,3},{6,4},{7,5},{8,6},{9,7},{10,8},{11,9},{12,... | collective-permute-start | bytes 442376 | tf_op jit(solution)/shard_map/ppermute | solution.py:230
  96.1 11.0 %collective-permute-start.9 = (bf16[2,144,256]{2,1,0:T(8,128)(2,1)S(1)}, bf16[2,144,256]{2,1,0:T(8,128)(2,1)S(1)}, u32[]{:S(2)}, u32[]{:S(2)}) collective-permute-start(bf16[2,144,256]{2,1,0:T(8,128)(2,1)S(1)} %get-tuple-element.6.args_1_), channel_id=1, source_target_pairs={{3,0},{4,1},{5,2},{6,3},{7,4},{8,5},{9,6},{10,7},{11,8},{12,9},{13... | collective-permute-start | bytes 442376 | tf_op jit(solution)/shard_map/ppermute | solution.py:230
  97.4 13.5 %collective-permute-start.10 = (bf16[2,144,256]{2,1,0:T(8,128)(2,1)S(1)}, bf16[2,144,256]{2,1,0:T(8,128)(2,1)S(1)}, u32[]{:S(2)}, u32[]{:S(2)}) collective-permute-start(bf16[2,144,256]{2,1,0:T(8,128)(2,1)S(1)} %get-tuple-element.6.args_1_), channel_id=1, source_target_pairs={{4,0},{5,1},{6,2},{7,3},{8,4},{9,5},{10,6},{11,7},{12,8},{13,9},{1... | collective-permute-start | bytes 442376 | tf_op jit(solution)/shard_map/ppermute | solution.py:230
  100.2 11.8 %copy-start.2 = (bf16[2304,256]{1,0:T(8,128)(2,1)S(1)}, bf16[2304,256]{1,0:T(8,128)(2,1)}, u32[]{:S(2)}) copy-start(bf16[2304,256]{1,0:T(8,128)(2,1)} %param.7) | copy-start | bytes 3538948
  100.2 11.8 %collective-permute-start.20 = (bf16[2,1,144,256]{3,2,1,0:T(8,128)(2,1)S(1)}, bf16[2,1,144,256]{3,2,1,0:T(8,128)(2,1)S(1)}, u32[]{:S(2)}, u32[]{:S(2)}) collective-permute-start(bf16[2,1,144,256]{3,2,1,0:T(8,128)(2,1)S(1)} %slice.24), channel_id=1, source_target_pairs={{0,32},{32,0},{64,96},{96,64},{128,160},{160,128},{192,224},{224,1... | collective-permute-start | bytes 442376 | tf_op jit(solution)/shard_map/ppermute | solution.py:270
